TPU v7x, 32 devices: a whole 2x2x4 slice. The times are simulated.
32 devices in a mesh: corpus: 4 (over z), rerank: 8 (over y, x, core).
Axes of the slice: x: 2, y: 2, z: 4, core: 2. Of those that a mesh axis runs over, the one named last changes fastest.
Arguments:
- store_rows: bfloat16 [128, 512, 3584], P('corpus', 'rerank'), may hold values from -400 to 400
- block_lengths: int32 [128], replicated, may hold values from 128 to 512
- queries: bfloat16 [32, 64, 3584], P(None, 'rerank'), may hold values from -400 to 400
- cand_owner: int32 [64, 1], replicated, may hold values from 0 to 3; in each aligned block of 16 rows (0 to 15, 16 to 31, ...) at most 5 rows name the same one
- cand_block: int32 [64], replicated, may hold values from 0 to 31
- cand_query: int32 [64], replicated, may hold values from 0 to 31
- norm_gain: bfloat16 [3584], replicated, may hold values from 0.099609375 to 1.8984375
- w_query: bfloat16 [3584, 1792], P('rerank'), may hold values from -8 to 8
- w_key: bfloat16 [3584, 256], P('rerank'), may hold values from -1 to 1
- w_value: bfloat16 [3584, 256], P('rerank'), may hold values from -0.09375 to 0.09375
- w_score: bfloat16 [1792], replicated, may hold values from -0.125 to 0.125
Outputs:
- passage_context: bfloat16 [80, 512, 1792], P('corpus', 'rerank')
- pair_scores: float32 [64], P(('corpus', 'rerank'))
Inputs may be any that keep to these rules, and one draw needn't show every extreme that they name: `cand_owner`: at most 5 of the 16 pairs of one corpus group (an aligned block of rows) name the same owner, in every draw, some group names one owner in exactly 5 of its 16 pairs.
All inputs are finite; a program needn't handle non-finite values.
Results may differ from a plain program's by a relative error of at most 0.013.
Values may be sent and summed in bfloat16 or wider, within the bound.
A program may use at most 128 MiB of HBM per device.

v0:
```python
import jax
import jax.numpy as jnp
from jax import lax
from jax.sharding import PartitionSpec as P

HDIM = 128
QHEADS = 14
KVHEADS = 2
BLK = 512
CAP = 5
ROPE_BASE = 1000000.0
EPSILON = 1e-06


def rotate(values, positions):
    head_dim = values.shape[-1]
    half_dim = head_dim // 2
    inverse = jnp.power(ROPE_BASE, -2.0 * jnp.arange(half_dim, dtype=jnp.float32) / head_dim)
    angles = positions.astype(jnp.float32)[..., None] * inverse
    cosine = jnp.cos(angles)[..., None, :]
    sine_part = jnp.sin(angles)[..., None, :]
    lower = values[..., :half_dim]
    upper = values[..., half_dim:]
    return jnp.concatenate(
        [lower * cosine - upper * sine_part, upper * cosine + lower * sine_part], axis=-1
    )


def pick_rows(table, wanted, indices):
    present = jnp.any(wanted, axis=1)
    picked = jnp.sum(jnp.where(wanted, indices[None, :], 0), axis=1)
    chosen = jnp.take(table, picked, axis=0)
    return jnp.where(present[:, None, None], chosen, jnp.zeros((), table.dtype))


def add_products(pieces, columns):
    return (
        jnp.dot(columns, pieces[0], preferred_element_type=jnp.float32),
        jnp.dot(columns, pieces[1], preferred_element_type=jnp.float32),
        jnp.dot(columns, pieces[2], preferred_element_type=jnp.float32),
    )


def attend_one(items):
    query_rot, key_rot, values, length = items
    seq_len = query_rot.shape[0]
    token_ids = jnp.arange(seq_len, dtype=jnp.int32)
    grouped = query_rot.reshape(seq_len, KVHEADS, QHEADS // KVHEADS, HDIM)
    logits = jnp.einsum(
        "skgd,tkd->kgst", grouped, key_rot, preferred_element_type=jnp.float32
    ) * HDIM ** (-0.5)
    live = (token_ids < length) | (token_ids >= BLK)
    allowed = live[None, :] & (token_ids[None, :] <= token_ids[:, None])
    masked = jnp.where(allowed, logits, -1e30)
    peak = jnp.max(masked, axis=-1, keepdims=True)
    weights = jnp.where(allowed, jnp.exp(masked - peak), 0.0)
    probs = (weights / jnp.sum(weights, axis=-1, keepdims=True)).astype(jnp.bfloat16)
    context = jnp.einsum("kgst,tkd->skgd", probs, values, preferred_element_type=jnp.float32)
    return context.reshape(seq_len, QHEADS * HDIM).astype(jnp.bfloat16)


def on_device(
    store_rows,
    block_lengths,
    queries,
    cand_owner,
    cand_block,
    cand_query,
    norm_gain,
    w_query,
    w_key,
    w_value,
    w_score,
):
    n_corpus = lax.axis_size("corpus")
    n_rerank = lax.axis_size("rerank")
    corpus_index = lax.axis_index("corpus")
    member = lax.axis_index("rerank")
    pair_total = cand_block.shape[0]
    pair_group = pair_total // n_corpus
    pair_dev = pair_group // n_rerank
    own_blocks = store_rows.shape[0]
    owners = cand_owner[:, 0]
    pair_order = jnp.arange(pair_total, dtype=jnp.int32)
    group_of = pair_order // pair_group
    earlier = (
        (owners[:, None] == owners[None, :])
        & (group_of[:, None] == group_of[None, :])
        & (pair_order[None, :] < pair_order[:, None])
    )
    owner_rank = jnp.sum(earlier.astype(jnp.int32), axis=1)
    slot_ids = jnp.arange(n_corpus * CAP, dtype=jnp.int32)
    slot_group = slot_ids // CAP
    slot_rank = slot_ids % CAP
    wanted = (
        (group_of[None, :] == slot_group[:, None])
        & (owners[None, :] == corpus_index)
        & (owner_rank[None, :] == slot_rank[:, None])
    )
    outgoing = pick_rows(store_rows, wanted, cand_block)
    arrived = lax.all_to_all(outgoing, "corpus", split_axis=0, concat_axis=0, tiled=True)
    local_pairs = corpus_index * pair_group + jnp.arange(pair_group, dtype=jnp.int32)
    local_owner = jnp.take(owners, local_pairs)
    local_rank = jnp.take(owner_rank, local_pairs)
    passages = jnp.take(arrived, local_owner * CAP + local_rank, axis=0)
    query_rows = jnp.take(queries, jnp.take(cand_query, local_pairs), axis=0)
    passage_rows, question_rows = (
        lax.all_to_all(passages, "rerank", split_axis=0, concat_axis=1, tiled=True),
        lax.all_to_all(query_rows, "rerank", split_axis=0, concat_axis=1, tiled=True),
    )
    joined = jnp.concatenate([passage_rows, question_rows], axis=1)
    device_pairs = (
        corpus_index * pair_group + member * pair_dev + jnp.arange(pair_dev, dtype=jnp.int32)
    )
    lengths = jnp.take(
        block_lengths,
        jnp.take(owners, device_pairs) * own_blocks + jnp.take(cand_block, device_pairs),
    )
    seq_len = joined.shape[1]
    width = joined.shape[2]
    row_count = pair_dev * seq_len
    widened = joined.astype(jnp.float32)
    inverse_rms = lax.rsqrt(jnp.mean(widened * widened, axis=-1, keepdims=True) + EPSILON)
    normed = (
        (widened * inverse_rms * norm_gain.astype(jnp.float32))
        .astype(jnp.bfloat16)
        .reshape(row_count, width)
    )
    query_raw, key_raw, value_raw = add_products(
        (
            lax.all_gather(w_query, "rerank", axis=0, tiled=True),
            lax.all_gather(w_key, "rerank", axis=0, tiled=True),
            lax.all_gather(w_value, "rerank", axis=0, tiled=True),
        ),
        normed,
    )
    token_ids = jnp.arange(seq_len, dtype=jnp.int32)
    positions = jnp.where(
        token_ids[None, :] < BLK, token_ids[None, :], lengths[:, None] + token_ids[None, :] - BLK
    )
    query_rot = rotate(query_raw.reshape(pair_dev, seq_len, QHEADS, HDIM), positions).astype(
        jnp.bfloat16
    )
    key_rot = rotate(key_raw.reshape(pair_dev, seq_len, KVHEADS, HDIM), positions).astype(
        jnp.bfloat16
    )
    values = value_raw.reshape(pair_dev, seq_len, KVHEADS, HDIM).astype(jnp.bfloat16)
    context = lax.map(attend_one, (query_rot, key_rot, values, lengths))
    pair_scores = jnp.dot(context[:, seq_len - 1, :], w_score, preferred_element_type=jnp.float32)
    keep = token_ids[None, :BLK] < lengths[:, None]
    passage_context = jnp.where(keep[:, :, None], context[:, :BLK], jnp.zeros((), jnp.bfloat16))
    returned = lax.all_to_all(passage_context, "rerank", split_axis=1, concat_axis=0, tiled=True)
    home_want = (local_owner[None, :] == slot_group[:, None]) & (
        local_rank[None, :] == slot_rank[:, None]
    )
    homebound = pick_rows(returned, home_want, jnp.arange(pair_group, dtype=jnp.int32))
    landed = lax.all_to_all(homebound, "corpus", split_axis=0, concat_axis=0, tiled=True)
    return (landed, pair_scores)


def solution(mesh):
    placed = (
        P("corpus", "rerank", None),
        P(),
        P(None, "rerank", None),
        P(),
        P(),
        P(),
        P(),
        P("rerank", None),
        P("rerank", None),
        P("rerank", None),
        P(),
    )
    return jax.shard_map(
        on_device,
        mesh=mesh,
        in_specs=placed,
        out_specs=(P("corpus", "rerank", None), P(("corpus", "rerank"))),
        check_vma=False,
    )
```

profile of v0, /device:TPU:2, one launch (start us, length us, event | category | flops | bytes accessed | tf_op | source)
XLA Modules:
  0.0 673.4 jit_solution(5403517321702879606)
XLA Ops:
  9.4 0.9 convert_reduce_fusion
  10.3 0.8 select_reduce_fusion
  11.4 11.1 %gather_fusion.1 = bf16[20,64,3584]{2,1,0:T(8,128)(2,1)} fusion(bf16[32,64,3584]{2,1,0:T(8,128)(2,1)} %param.17, s32[1024]{0:T(1024)S(1)} %pad_clamp_fusion.3), kind=kCustom, calls=%fused_computation.6 | custom fusion | bytes 18350160 | tf_op jit(solution)/shard_map/jit(_take)/gather | solution.py:32
  22.5 8.2 %select_select_fusion = bf16[20,64,3584]{2,1,0:T(8,128)(2,1)} fusion(bf16[20,64,3584]{2,1,0:T(8,128)(2,1)} %gather_fusion.1, pred[20]{0:T(512)(128)(4,1)S(1)} %compare_and_fusion.5, pred[20]{0:T(512)(128)(4,1)S(1)} %fusion.35), kind=kLoop, calls=%fused_computation.45 | loop fusion | flops 9175040 | bytes 18350120 | tf_op jit(solution)/shard_map/jit(_where)/select_n | solution.py:33
  30.7 5.9 all-to-all-start
  40.6 1.1 broadcast_select_fusion.2
  41.7 195.2 %all-to-all-done = bf16[20,64,3584]{2,1,0:T(8,128)(2,1)} async-done(((bf16[20,64,3584]{2,1,0:T(8,128)(2,1)}), bf16[20,64,3584]{2,1,0:T(8,128)(2,1)}, u32[]{:S(2)}, u32[]{:S(2)}) %all-to-all-start) | async-done | bytes 9175072 | tf_op jit(solution)/shard_map/all_to_all | solution.py:101
  236.8 4.2 all-to-all-start.2
  241.1 7.6 %gather_fusion.2 = bf16[16,64,3584]{2,1,0:T(8,128)(2,1)} fusion(bf16[20,64,3584]{2,1,0:T(8,128)(2,1)} %all-to-all-done, s32[1024]{0:T(1024)S(1)} %pad_clamp_fusion.2), kind=kCustom, calls=%fused_computation.7 | custom fusion | bytes 14680128 | tf_op jit(solution)/shard_map/jit(_take)/gather | solution.py:105
  248.7 6.9 %broadcast_select_fusion = bf16[16,64,3584]{2,1,0:T(8,128)(2,1)} fusion(bf16[16,64,3584]{2,1,0:T(8,128)(2,1)} %gather_fusion.2, pred[16]{0:T(512)(128)(4,1)S(1)} %get-tuple-element.63), kind=kLoop, calls=%fused_computation.50 | loop fusion | flops 3670016 | bytes 14680080 | tf_op jit(solution)/shard_map/jit(_take)/select_n | solution.py:105
  255.6 5.2 all-to-all-start.1
  263.7 2.1 multiply_cosine_fusion
  265.8 1.0 copy.62
  266.8 3.8 copy.49
  270.6 3.8 copy.48
  274.4 67.8 %all-to-all-done.1 = bf16[16,64,3584]{2,1,0:T(8,128)(2,1)} async-done(((bf16[16,64,3584]{2,1,0:T(8,128)(2,1)}), bf16[16,64,3584]{2,1,0:T(8,128)(2,1)}, u32[]{:S(2)}, u32[]{:S(2)}) %all-to-all-start.1) | async-done | bytes 7340064 | tf_op jit(solution)/shard_map/all_to_all | solution.py:108
  342.2 3.8 copy.46
  346.0 2.0 fusion.30
  348.9 2.4 fusion.41
  352.1 3.4 convolution_convert_fusion
  355.5 18.0 %copy.50 = bf16[1792,3584]{1,0:T(8,128)(2,1)} copy(bf16[1792,3584]{0,1:T(8,128)(2,1)} %bitcast.115) | data formatting | bytes 25690112 | tf_op jit(solution)/shard_map/dot_general | solution.py:38
  373.5 23.9 %fusion.39 = f32[2,576,14,128]{3,1,2,0:T(8,128)} fusion(bf16[14,128,3584,1]{2,1,0,3:T(8,128)(2,1)} %bitcast.116, f32[3584]{0:T(1024)S(1)} %convert_element_type.66, f32[2,576]{1,0:T(2,128)S(1)} %add_rsqrt_fusion, bf16[2,64,3584]{2,1,0:T(8,128)(2,1)S(1)} %bitcast.121, bf16[2,512,3584]{2,1,0:T(8,128)(2,1)} %bitcast.112), kind=kOutput, calls=%fused_computation.117 | convolution fusion | flops 14826405888 | bytes 29379072 | tf_op jit(solution)/shard_map/dot_general | solution.py:38
  397.4 8.6 %subtract_convert_fusion = (bf16[2,576,14,64]{3,1,2,0:T(8,128)(2,1)S(1)}, bf16[2,576,14,64]{3,1,2,0:T(8,128)(2,1)S(1)}) fusion(f32[2,576,14,128]{3,1,2,0:T(8,128)} %fusion.39, f32[2,576,64]{2,1,0:T(8,128)S(1)} %get-tuple-element.62, f32[2,576,64]{2,1,0:T(8,128)S(1)} %get-tuple-element.61), kind=kLoop, calls=%fused_computation.49 | loop fusion | flops 8257536 | bytes 12976128 | tf_op jit(solution)/shard_map/convert.2
  405.9 4.3 pad_maximum_fusion.1
  410.2 69.3 %while.10 = (s32[]{:T(128)}, bf16[2,576,1792]{2,1,0:T(8,128)(2,1)}, bf16[2,576,2,128]{3,1,2,0:T(8,128)(2,1)}, s32[2]{0:T(128)S(1)}, bf16[2,576,2,128]{3,1,2,0:T(...) while((s32[]{:T(128)}, bf16[2,576,1792]{2,1,0:T(8,128)(2,1)}, ...), condition=%wide.region_9.12_spmd, body=%wide.region_6.11_spmd.sunk | while | flops 2412382464 | bytes 61592804 | solution.py:148
  410.4 1.7 constant_dynamic-slice_fusion.2
  413.5 12.5 %fusion.66 = (f32[2,7,576]{2,1,0:T(8,128)S(1)}, f32[2,7,576,576]{2,3,1,0:T(8,128)}) fusion(pred[576,576]{0,1:T(8,128)(4,1)S(1)} %fusion.65, bf16[576,2,7,128]{3,0,2,1:T(8,128)(2,1)S(1)} %bitcast.108, bf16[2,576,2,128]{3,1,2,0:T(8,128)(2,1)S(1)} %get-tuple-element.128, s32[]{:T(128)} %get-tuple-element.117), kind=kOutput, calls=%fused_computation.119.clone.1 | convolution fusion | flops 1212310016 | bytes 21708292 | tf_op jit(solution)/shard_map/while/body/eval_jaxpr/sub | solution.py:56
  426.0 11.1 %convert_bitcast_fusion.2 = bf16[576,2,7,128]{3,0,2,1:T(8,128)(2,1)S(1)} fusion(f32[2,7,576,576]{2,3,1,0:T(8,128)} %get-tuple-element.108, f32[2,7,576]{2,1,0:T(8,128)S(1)} %get-tuple-element.109, bf16[2,576,2,128]{3,1,2,0:T(8,128)(2,1)} %get-tuple-element.126, s32[]{:T(128)} %get-tuple-element.117), kind=kOutput, calls=%fused_computation.19.clone.1 | convolution fusion | flops 1199407104 | bytes 23035904 | tf_op jit(solution)/shard_map/while/body/eval_jaxpr/kgst,tkd->skgd/dot_general | solution.py:58
  437.1 1.4 copy.64
  438.5 3.3 convert_element_type.102
  441.8 3.0 constant_dynamic-update-slice_fusion.2
  444.8 1.7 constant_dynamic-slice_fusion.2
  448.0 12.5 %fusion.66 = (f32[2,7,576]{2,1,0:T(8,128)S(1)}, f32[2,7,576,576]{2,3,1,0:T(8,128)}) fusion(pred[576,576]{0,1:T(8,128)(4,1)S(1)} %fusion.65, bf16[576,2,7,128]{3,0,2,1:T(8,128)(2,1)S(1)} %bitcast.108, bf16[2,576,2,128]{3,1,2,0:T(8,128)(2,1)S(1)} %get-tuple-element.128, s32[]{:T(128)} %get-tuple-element.117), kind=kOutput, calls=%fused_computation.119.clone.1 | convolution fusion | flops 1212310016 | bytes 21708292 | tf_op jit(solution)/shard_map/while/body/eval_jaxpr/sub | solution.py:56
  460.5 11.1 %convert_bitcast_fusion.2 = bf16[576,2,7,128]{3,0,2,1:T(8,128)(2,1)S(1)} fusion(f32[2,7,576,576]{2,3,1,0:T(8,128)} %get-tuple-element.108, f32[2,7,576]{2,1,0:T(8,128)S(1)} %get-tuple-element.109, bf16[2,576,2,128]{3,1,2,0:T(8,128)(2,1)} %get-tuple-element.126, s32[]{:T(128)} %get-tuple-element.117), kind=kOutput, calls=%fused_computation.19.clone.1 | convolution fusion | flops 1199407104 | bytes 23035904 | tf_op jit(solution)/shard_map/while/body/eval_jaxpr/kgst,tkd->skgd/dot_general | solution.py:58
  471.6 1.4 copy.64
  473.0 3.3 convert_element_type.102
  476.3 3.0 constant_dynamic-update-slice_fusion.2
  479.5 6.4 copy.51
  486.0 5.7 broadcast_select_fusion.1
  491.7 5.9 all-to-all-start.3
  497.8 41.8 %all-to-all-done.3 = bf16[2,512,1792]{2,0,1:T(2,128)(2,1)} async-done(((bf16[2,512,1792]{2,0,1:T(2,128)(2,1)}), bf16[2,512,1792]{2,0,1:T(2,128)(2,1)}, u32[]{:S(2)}, u32[]{:S(2)}) %all-to-all-start.3) | async-done | bytes 3670048 | tf_op jit(solution)/shard_map/all_to_all | solution.py:152
  539.7 2.5 copy.52
  542.2 2.1 copy.53
  544.3 5.3 gather_fusion.4
  549.5 5.1 select_select_fusion.1
  554.7 4.9 all-to-all-start.4
  561.1 100.6 %all-to-all-done.4 = bf16[20,64,1792]{2,1,0:T(8,128)(2,1)} async-done(((bf16[20,64,1792]{2,1,0:T(8,128)(2,1)}), bf16[20,64,1792]{2,1,0:T(8,128)(2,1)}, u32[]{:S(2)}, u32[]{:S(2)}) %all-to-all-start.4) | async-done | bytes 4587552 | tf_op jit(solution)/shard_map/all_to_all | solution.py:157
  661.8 4.9 copy.75
  (97 shorter events, 15.3 us)
Async XLA Ops:
  7.2 32.8 %copy-start = (bf16[32,8,3584]{2,1,0:T(8,128)(2,1)S(1)}, bf16[32,8,3584]{2,1,0:T(8,128)(2,1)}, u32[]{:S(2)}) copy-start(bf16[32,8,3584]{2,1,0:T(8,128)(2,1)} %param.19) | copy-start | bytes 5505028
  7.2 259.6 %all-gather.6.cloned.1.call-start = ((), (), s32[]{:S(2)}) async-start(), calls=%async_computation.6 | async-start | bytes 2064384 | tf_op jit(solution)/shard_map/all_gather | solution.py:132
  7.9 262.7 %all-gather.4.cloned.1.call-start = ((), (), s32[]{:S(2)}) async-start(), calls=%async_computation.5 | async-start | bytes 2064384 | tf_op jit(solution)/shard_map/all_gather | solution.py:133
  8.7 13.8 %copy-start.12 = (s32[20]{0:T(128)}, s32[20]{0:T(128)S(1)}, u32[]{:S(2)}) copy-start(s32[20]{0:T(128)S(1)} %get-tuple-element.67) | copy-start | bytes 244
  8.7 13.8 %copy-start.14 = (s32[20]{0:T(128)}, s32[20]{0:T(128)S(1)}, u32[]{:S(2)}) copy-start(s32[20]{0:T(128)S(1)} %get-tuple-element.68) | copy-start | bytes 244
  30.7 7.3 %copy-start.2 = (s32[64,1]{0,1:T(1,128)S(1)}, s32[64,1]{0,1:T(1,128)}, u32[]{:S(2)}) copy-start(s32[64,1]{0,1:T(1,128)} %param.20) | copy-start | bytes 772
  30.7 8.0 %copy-start.4 = (s32[64]{0:T(128)S(1)}, s32[64]{0:T(128)}, u32[]{:S(2)}) copy-start(s32[64]{0:T(128)} %param.22) | copy-start | bytes 772
  30.7 206.1 %all-to-all-start = ((bf16[20,64,3584]{2,1,0:T(8,128)(2,1)}), bf16[20,64,3584]{2,1,0:T(8,128)(2,1)}, u32[]{:S(2)}, u32[]{:S(2)}) async-start(bf16[20,64,3584]{2,1,0:T(8,128)(2,1)} %select_select_fusion), calls=%async_computation | async-start | bytes 18350080 | tf_op jit(solution)/shard_map/all_to_all | solution.py:101
  36.6 318.9 %all-gather.8.cloned.1.call-start = ((), (), s32[]{:S(2)}) async-start(), calls=%async_computation.7 | async-start | bytes 14450688 | tf_op jit(solution)/shard_map/all_gather | solution.py:131
  236.8 18.7 %all-to-all-start.2 = ((bf16[16,8,3584]{2,1,0:T(8,128)(2,1)}), bf16[16,8,3584]{2,1,0:T(8,128)(2,1)S(1)}, u32[]{:S(2)}, u32[]{:S(2)}) async-start(bf16[16,8,3584]{2,1,0:T(8,128)(2,1)} %broadcast_select_fusion.2), calls=%async_computation.2 | async-start | bytes 1835008 | tf_op jit(solution)/shard_map/all_to_all | solution.py:109
  255.6 5.9 copy-start.3
  255.6 6.6 copy-start.11
  255.6 6.6 copy-start.5
  255.6 86.6 %all-to-all-start.1 = ((bf16[16,64,3584]{2,1,0:T(8,128)(2,1)}), bf16[16,64,3584]{2,1,0:T(8,128)(2,1)}, u32[]{:S(2)}, u32[]{:S(2)}) async-start(bf16[16,64,3584]{2,1,0:T(8,128)(2,1)} %broadcast_select_fusion), calls=%async_computation.1 | async-start | bytes 14680064 | tf_op jit(solution)/shard_map/all_to_all | solution.py:108
  342.2 3.8 copy-start.7
  346.0 6.1 copy-start.6
  346.0 2.9 copy-start.9
  348.9 3.2 copy-start.8
  479.5 6.5 copy-start.10
  486.0 11.6 %copy-start.13 = (s32[20]{0:T(128)S(1)}, s32[20]{0:T(128)}, u32[]{:S(2)}) copy-start(s32[20]{0:T(128)} %copy-done.12) | copy-start | bytes 244
  486.0 11.6 %copy-start.15 = (s32[20]{0:T(128)S(1)}, s32[20]{0:T(128)}, u32[]{:S(2)}) copy-start(s32[20]{0:T(128)} %copy-done.14) | copy-start | bytes 244
  486.0 11.6 %copy-start.16 = (s32[16]{0:T(128)S(1)}, s32[16]{0:T(128)}, u32[]{:S(2)}) copy-start(s32[16]{0:T(128)} %get-tuple-element.65) | copy-start | bytes 196
  486.0 11.6 %copy-start.17 = (s32[16]{0:T(128)S(1)}, s32[16]{0:T(128)}, u32[]{:S(2)}) copy-start(s32[16]{0:T(128)} %get-tuple-element.66) | copy-start | bytes 196
  491.7 48.0 %all-to-all-start.3 = ((bf16[2,512,1792]{2,0,1:T(2,128)(2,1)}), bf16[2,512,1792]{2,0,1:T(2,128)(2,1)}, u32[]{:S(2)}, u32[]{:S(2)}) async-start(bf16[2,512,1792]{2,0,1:T(2,128)(2,1)} %broadcast_select_fusion.1), calls=%async_computation.3 | async-start | bytes 7340032 | tf_op jit(solution)/shard_map/all_to_all | solution.py:152
  549.5 10.1 %copy-start.18 = (bf16[1792]{0:T(1024)(128)(2,1)S(1)}, bf16[1792]{0:T(1024)(128)(2,1)}, u32[]{:S(2)}) copy-start(bf16[1792]{0:T(1024)(128)(2,1)} %param.27) | copy-start | bytes 10756
  549.5 117.1 %copy-start.1 = (bf16[32,8,3584]{2,1,0:T(8,128)(2,1)S(1)}, bf16[32,8,3584]{2,1,0:T(8,128)(2,1)}, u32[]{:S(2)}) copy-start(bf16[32,8,3584]{2,1,0:T(8,128)(2,1)} %param.19) | copy-start | bytes 5505028
  554.7 107.1 %all-to-all-start.4 = ((bf16[20,64,1792]{2,1,0:T(8,128)(2,1)}), bf16[20,64,1792]{2,1,0:T(8,128)(2,1)}, u32[]{:S(2)}, u32[]{:S(2)}) async-start(bf16[20,64,1792]{2,1,0:T(8,128)(2,1)} %select_select_fusion.1), calls=%async_computation.4 | async-start | bytes 9175040 | tf_op jit(solution)/shard_map/all_to_all | solution.py:157
Sparse Core Ops, SparseCore 0:
  9.9 27.8 all-gather.5
  39.7 26.6 all-gather.3
  68.3 73.0 all-gather.7
where the time goes:
time: 679 us; the launch traced here: 673 us
  waiting for transfers between devices  407 us (60%)
  local copies, waits for them, and re-layouts  96.6 us (14%)
  matrix products  77.5 us (11%)
  other arithmetic  50.7 us (7%)
  starting transfers between devices  26.3 us (4%)
  between operations  14.4 us (2%)
    all_to_all x1, waiting for transfers between devices, on_device(): lax.all_to_all(outgoing, 'corpus', split_axis=0, concat_axis=0, tiled=True)  195 us
    all_to_all x1, waiting for transfers between devices, on_device(): lax.all_to_all(homebound, 'corpus', split_axis=0, concat_axis=0, tiled=True)  101 us
    all_to_all x1, waiting for transfers between devices, on_device(): lax.all_to_all(passages, 'rerank', split_axis=0, concat_axis=1, tiled=True)  67.8 us
    all_to_all x1, waiting for transfers between devices, on_device(): lax.all_to_all(passage_context, 'rerank', split_axis=1, concat_axis=0, ti...  41.8 us
    sub x2, matrix products, attend_one(): weights = jnp.where(allowed, jnp.exp(masked - peak), 0.0)  25 us
    dot_general x1, matrix products, add_products(): jnp.dot(columns, pieces[0], preferred_element_type=jnp.float32)  23.9 us
    dot_general x2, matrix products, attend_one(): jnp.einsum('kgst,tkd->skgd', probs, values, preferred_element_type=jnp.fl...  22.2 us
    dot_general x1, local copies, waits for them, and re-layouts, add_products(): jnp.dot(columns, pieces[0], preferred_element_type=jnp.float32)  18 us
  transfers between devices with their start and end apart: 8, of which 4 were waited for; matrix products, arithmetic and copies ran while one was open for 10% of the time, Pallas kernels for 0%

commit v1 on v0

--- a/solution.py
+++ b/solution.py
@@ -1,3 +1,4 @@
+import functools
 import jax
 import jax.numpy as jnp
 from jax import lax
@@ -10,6 +11,29 @@
 CAP = 5
 ROPE_BASE = 1000000.0
 EPSILON = 1e-06
+
+
+def _prepare_modes(x_local, axis_key):
+    f_next, answer = (lax.axis_size(axis_key), lax.axis_index(axis_key))
+    latest = x_local.shape[0] // f_next
+    f_now = list(x_local.shape)
+    f_now[0] = latest
+    item_now = f_now[0]
+    f_now[0] = item_now * f_next
+    to_i = 0
+    carry = jnp.zeros(f_now, x_local.dtype)
+    while to_i < f_next:
+        clean = lax.dynamic_slice_in_dim(x_local, (answer ^ to_i) * latest, latest, axis=0)
+        if to_i:
+            clean = lax.ppermute(
+                clean, axis_name=axis_key, perm=[(ii, ii ^ to_i) for ii in range(f_next)]
+            )
+        carry = lax.dynamic_update_slice_in_dim(carry, clean, (answer ^ to_i) * item_now, axis=0)
+        to_i += 1
+    return carry
+
+
+create_surface = functools.partial(_prepare_modes, axis_key="corpus")
 
 
 def rotate(values, positions):
@@ -154,7 +178,7 @@
         local_rank[None, :] == slot_rank[:, None]
     )
     homebound = pick_rows(returned, home_want, jnp.arange(pair_group, dtype=jnp.int32))
-    landed = lax.all_to_all(homebound, "corpus", split_axis=0, concat_axis=0, tiled=True)
+    landed = create_surface(homebound)
     return (landed, pair_scores)
 
 

time: 679 us -> 670 us (0.987)
  the two profiles are of different devices: /device:TPU:2 before, /device:TPU:10 now
where the time goes in v1:
time: 670 us; the launch traced here: 664 us
  waiting for transfers between devices  401 us (60%)
  local copies, waits for them, and re-layouts  95.8 us (14%)
  matrix products  77.5 us (12%)
  other arithmetic  48.4 us (7%)
  starting transfers between devices  26.7 us (4%)
  between operations  14.4 us (2%)
    all_to_all x1, waiting for transfers between devices, on_device(): lax.all_to_all(outgoing, 'corpus', split_axis=0, concat_axis=0, tiled=True)  192 us
    ppermute x3, waiting for transfers between devices, _prepare_modes(): lax.ppermute(clean, axis_name=axis_key, perm=[(ii, ii ^ to_i) for ii in r...  97.3 us
    all_to_all x1, waiting for transfers between devices, on_device(): lax.all_to_all(passages, 'rerank', split_axis=0, concat_axis=1, tiled=True)  67.7 us
    all_to_all x1, waiting for transfers between devices, on_device(): lax.all_to_all(passage_context, 'rerank', split_axis=1, concat_axis=0, ti...  41.8 us
    sub x2, matrix products, attend_one(): weights = jnp.where(allowed, jnp.exp(masked - peak), 0.0)  25 us
    dot_general x1, matrix products, add_products(): jnp.dot(columns, pieces[0], preferred_element_type=jnp.float32)  23.9 us
    dot_general x2, matrix products, attend_one(): jnp.einsum('kgst,tkd->skgd', probs, values, preferred_element_type=jnp.fl...  22.2 us
    dot_general x1, local copies, waits for them, and re-layouts, add_products(): jnp.dot(columns, pieces[0], preferred_element_type=jnp.float32)  18 us
  transfers between devices with their start and end apart: 10, of which 6 were waited for; matrix products, arithmetic and copies ran while one was open for 10% of the time, Pallas kernels for 0%

profile of v1, /device:TPU:10, one launch (start us, length us, event | category | flops | bytes accessed | tf_op | source)
XLA Modules:
  0.0 664.0 jit_solution(15614570440842747529)
XLA Ops:
  11.4 11.1 %gather_fusion.1 = bf16[20,64,3584]{2,1,0:T(8,128)(2,1)} fusion(bf16[32,64,3584]{2,1,0:T(8,128)(2,1)} %param.17, s32[1024]{0:T(1024)S(1)} %pad_clamp_fusion.3), kind=kCustom, calls=%fused_computation.6 | custom fusion | bytes 18350160 | tf_op jit(solution)/shard_map/jit(_take)/gather | solution.py:56
  22.5 8.2 %select_select_fusion = bf16[20,64,3584]{2,1,0:T(8,128)(2,1)} fusion(bf16[20,64,3584]{2,1,0:T(8,128)(2,1)} %gather_fusion.1, pred[20]{0:T(512)(128)(4,1)S(1)} %compare_and_fusion.5, pred[20]{0:T(512)(128)(4,1)S(1)} %fusion.35), kind=kLoop, calls=%fused_computation.45 | loop fusion | flops 9175040 | bytes 18350120 | tf_op jit(solution)/shard_map/jit(_where)/select_n | solution.py:57
  30.7 6.3 all-to-all-start
  41.0 1.1 broadcast_select_fusion.2
  42.0 191.8 %all-to-all-done = bf16[20,64,3584]{2,1,0:T(8,128)(2,1)} async-done(((bf16[20,64,3584]{2,1,0:T(8,128)(2,1)}), bf16[20,64,3584]{2,1,0:T(8,128)(2,1)}, u32[]{:S(2)}, u32[]{:S(2)}) %all-to-all-start) | async-done | bytes 9175072 | tf_op jit(solution)/shard_map/all_to_all | solution.py:125
  233.9 4.2 all-to-all-start.2
  238.1 7.6 %gather_fusion.2 = bf16[16,64,3584]{2,1,0:T(8,128)(2,1)} fusion(bf16[20,64,3584]{2,1,0:T(8,128)(2,1)} %all-to-all-done, s32[1024]{0:T(1024)S(1)} %pad_clamp_fusion.2), kind=kCustom, calls=%fused_computation.7 | custom fusion | bytes 14680128 | tf_op jit(solution)/shard_map/jit(_take)/gather | solution.py:129
  245.7 6.8 %broadcast_select_fusion = bf16[16,64,3584]{2,1,0:T(8,128)(2,1)} fusion(bf16[16,64,3584]{2,1,0:T(8,128)(2,1)} %gather_fusion.2, pred[16]{0:T(512)(128)(4,1)S(1)} %get-tuple-element.67), kind=kLoop, calls=%fused_computation.50 | loop fusion | flops 3670016 | bytes 14680080 | tf_op jit(solution)/shard_map/jit(_take)/select_n | solution.py:129
  252.6 5.2 all-to-all-start.1
  260.7 2.1 multiply_cosine_fusion
  263.8 3.8 copy.49
  267.7 3.8 copy.48
  271.5 67.7 %all-to-all-done.1 = bf16[16,64,3584]{2,1,0:T(8,128)(2,1)} async-done(((bf16[16,64,3584]{2,1,0:T(8,128)(2,1)}), bf16[16,64,3584]{2,1,0:T(8,128)(2,1)}, u32[]{:S(2)}, u32[]{:S(2)}) %all-to-all-start.1) | async-done | bytes 7340064 | tf_op jit(solution)/shard_map/all_to_all | solution.py:132
  339.2 3.8 copy.46
  343.0 2.0 fusion.30
  345.9 2.4 fusion.41
  349.8 3.4 convolution_convert_fusion
  353.2 18.0 %copy.50 = bf16[1792,3584]{1,0:T(8,128)(2,1)} copy(bf16[1792,3584]{0,1:T(8,128)(2,1)} %bitcast.115) | data formatting | bytes 25690112 | tf_op jit(solution)/shard_map/dot_general | solution.py:62
  371.1 23.9 %fusion.39 = f32[2,576,14,128]{3,1,2,0:T(8,128)} fusion(bf16[14,128,3584,1]{2,1,0,3:T(8,128)(2,1)} %bitcast.116, f32[3584]{0:T(1024)S(1)} %convert_element_type.66, f32[2,576]{1,0:T(2,128)S(1)} %add_rsqrt_fusion, bf16[2,64,3584]{2,1,0:T(8,128)(2,1)S(1)} %bitcast.121, bf16[2,512,3584]{2,1,0:T(8,128)(2,1)} %bitcast.112), kind=kOutput, calls=%fused_computation.124 | convolution fusion | flops 14826405888 | bytes 29379072 | tf_op jit(solution)/shard_map/dot_general | solution.py:62
  395.0 8.6 %subtract_convert_fusion = (bf16[2,576,14,64]{3,1,2,0:T(8,128)(2,1)S(1)}, bf16[2,576,14,64]{3,1,2,0:T(8,128)(2,1)S(1)}) fusion(f32[2,576,14,128]{3,1,2,0:T(8,128)} %fusion.39, f32[2,576,64]{2,1,0:T(8,128)S(1)} %get-tuple-element.66, f32[2,576,64]{2,1,0:T(8,128)S(1)} %get-tuple-element.65), kind=kLoop, calls=%fused_computation.49 | loop fusion | flops 8257536 | bytes 12976128 | tf_op jit(solution)/shard_map/convert.2
  403.6 4.3 pad_maximum_fusion.1
  407.9 69.3 %while.10 = (s32[]{:T(128)}, bf16[2,576,1792]{2,1,0:T(8,128)(2,1)}, bf16[2,576,2,128]{3,1,2,0:T(8,128)(2,1)}, s32[2]{0:T(128)S(1)}, bf16[2,576,2,128]{3,1,2,0:T(...) while((s32[]{:T(128)}, bf16[2,576,1792]{2,1,0:T(8,128)(2,1)}, ...), condition=%wide.region_9.12_spmd, body=%wide.region_6.11_spmd.sunk | while | flops 2412382464 | bytes 61592804 | solution.py:172
  408.0 1.7 constant_dynamic-slice_fusion.5
  411.2 12.5 %fusion.66 = (f32[2,7,576]{2,1,0:T(8,128)S(1)}, f32[2,7,576,576]{2,3,1,0:T(8,128)}) fusion(pred[576,576]{0,1:T(8,128)(4,1)S(1)} %fusion.65, bf16[576,2,7,128]{3,0,2,1:T(8,128)(2,1)S(1)} %bitcast.108, bf16[2,576,2,128]{3,1,2,0:T(8,128)(2,1)S(1)} %get-tuple-element.132, s32[]{:T(128)} %get-tuple-element.121), kind=kOutput, calls=%fused_computation.126.clone.1 | convolution fusion | flops 1212310016 | bytes 21708292 | tf_op jit(solution)/shard_map/while/body/eval_jaxpr/sub | solution.py:80
  423.7 11.1 %convert_bitcast_fusion.2 = bf16[576,2,7,128]{3,0,2,1:T(8,128)(2,1)S(1)} fusion(f32[2,7,576,576]{2,3,1,0:T(8,128)} %get-tuple-element.112, f32[2,7,576]{2,1,0:T(8,128)S(1)} %get-tuple-element.113, bf16[2,576,2,128]{3,1,2,0:T(8,128)(2,1)} %get-tuple-element.130, s32[]{:T(128)} %get-tuple-element.121), kind=kOutput, calls=%fused_computation.19.clone.1 | convolution fusion | flops 1199407104 | bytes 23035904 | tf_op jit(solution)/shard_map/while/body/eval_jaxpr/kgst,tkd->skgd/dot_general | solution.py:82
  434.8 1.4 copy.64
  436.2 3.3 convert_element_type.102
  439.5 3.0 constant_dynamic-update-slice_fusion.5
  442.5 1.7 constant_dynamic-slice_fusion.5
  445.7 12.5 %fusion.66 = (f32[2,7,576]{2,1,0:T(8,128)S(1)}, f32[2,7,576,576]{2,3,1,0:T(8,128)}) fusion(pred[576,576]{0,1:T(8,128)(4,1)S(1)} %fusion.65, bf16[576,2,7,128]{3,0,2,1:T(8,128)(2,1)S(1)} %bitcast.108, bf16[2,576,2,128]{3,1,2,0:T(8,128)(2,1)S(1)} %get-tuple-element.132, s32[]{:T(128)} %get-tuple-element.121), kind=kOutput, calls=%fused_computation.126.clone.1 | convolution fusion | flops 1212310016 | bytes 21708292 | tf_op jit(solution)/shard_map/while/body/eval_jaxpr/sub | solution.py:80
  458.2 11.1 %convert_bitcast_fusion.2 = bf16[576,2,7,128]{3,0,2,1:T(8,128)(2,1)S(1)} fusion(f32[2,7,576,576]{2,3,1,0:T(8,128)} %get-tuple-element.112, f32[2,7,576]{2,1,0:T(8,128)S(1)} %get-tuple-element.113, bf16[2,576,2,128]{3,1,2,0:T(8,128)(2,1)} %get-tuple-element.130, s32[]{:T(128)} %get-tuple-element.121), kind=kOutput, calls=%fused_computation.19.clone.1 | convolution fusion | flops 1199407104 | bytes 23035904 | tf_op jit(solution)/shard_map/while/body/eval_jaxpr/kgst,tkd->skgd/dot_general | solution.py:82
  469.3 1.4 copy.64
  470.6 3.3 convert_element_type.102
  474.0 3.0 constant_dynamic-update-slice_fusion.5
  477.2 6.4 copy.51
  483.6 5.7 broadcast_select_fusion.1
  489.3 5.9 all-to-all-start.3
  495.5 41.8 %all-to-all-done.3 = bf16[2,512,1792]{2,0,1:T(2,128)(2,1)} async-done(((bf16[2,512,1792]{2,0,1:T(2,128)(2,1)}), bf16[2,512,1792]{2,0,1:T(2,128)(2,1)}, u32[]{:S(2)}, u32[]{:S(2)}) %all-to-all-start.3) | async-done | bytes 3670048 | tf_op jit(solution)/shard_map/all_to_all | solution.py:176
  537.3 2.5 copy.52
  539.8 2.1 copy.53
  541.9 5.3 gather_fusion.4
  547.2 2.9 select_select_fusion.1
  551.0 3.5 collective-permute-start
  554.5 1.5 collective-permute-start.2
  557.5 45.1 %collective-permute-done = bf16[5,64,1792]{2,1,0:T(8,128)(2,1)S(1)} collective-permute-done((bf16[5,64,1792]{2,1,0:T(8,128)(2,1)S(1)}, bf16[5,64,1792]{2,1,0:T(8,128)(2,1)S(1)}, u32[]{:S(2)}, u32[]{:S(2)}) %collective-permute-start) | collective-permute-done | bytes 1146912 | tf_op jit(solution)/shard_map/ppermute | solution.py:28
  602.7 26.7 %collective-permute-done.1 = bf16[5,64,1792]{2,1,0:T(8,128)(2,1)S(1)} collective-permute-done((bf16[5,64,1792]{2,1,0:T(8,128)(2,1)S(1)}, bf16[5,64,1792]{2,1,0:T(8,128)(2,1)S(1)}, u32[]{:S(2)}, u32[]{:S(2)}) %collective-permute-start.1) | collective-permute-done | bytes 1146912 | tf_op jit(solution)/shard_map/ppermute | solution.py:28
  629.5 25.5 %collective-permute-done.2 = bf16[5,64,1792]{2,1,0:T(8,128)(2,1)S(1)} collective-permute-done((bf16[5,64,1792]{2,1,0:T(8,128)(2,1)S(1)}, bf16[5,64,1792]{2,1,0:T(8,128)(2,1)S(1)}, u32[]{:S(2)}, u32[]{:S(2)}) %collective-permute-start.2) | collective-permute-done | bytes 1146912 | tf_op jit(solution)/shard_map/ppermute | solution.py:28
  655.1 2.1 copy-done.7
  (107 shorter events, 20.0 us)
Async XLA Ops:
  7.2 33.2 %copy-start = (bf16[32,8,3584]{2,1,0:T(8,128)(2,1)S(1)}, bf16[32,8,3584]{2,1,0:T(8,128)(2,1)}, u32[]{:S(2)}) copy-start(bf16[32,8,3584]{2,1,0:T(8,128)(2,1)} %param.19) | copy-start | bytes 5505028
  7.2 256.7 %all-gather.6.cloned.1.call-start = ((), (), s32[]{:S(2)}) async-start(), calls=%async_computation.5 | async-start | bytes 2064384 | tf_op jit(solution)/shard_map/all_gather | solution.py:156
  7.9 259.8 %all-gather.4.cloned.1.call-start = ((), (), s32[]{:S(2)}) async-start(), calls=%async_computation.4 | async-start | bytes 2064384 | tf_op jit(solution)/shard_map/all_gather | solution.py:157
  8.7 13.8 %copy-start.13 = (s32[20]{0:T(128)}, s32[20]{0:T(128)S(1)}, u32[]{:S(2)}) copy-start(s32[20]{0:T(128)S(1)} %get-tuple-element.71) | copy-start | bytes 244
  8.7 13.8 %copy-start.15 = (s32[20]{0:T(128)}, s32[20]{0:T(128)S(1)}, u32[]{:S(2)}) copy-start(s32[20]{0:T(128)S(1)} %get-tuple-element.72) | copy-start | bytes 244
  30.7 7.7 %copy-start.2 = (s32[64,1]{0,1:T(1,128)S(1)}, s32[64,1]{0,1:T(1,128)}, u32[]{:S(2)}) copy-start(s32[64,1]{0,1:T(1,128)} %param.20) | copy-start | bytes 772
  30.7 8.3 %copy-start.4 = (s32[64]{0:T(128)S(1)}, s32[64]{0:T(128)}, u32[]{:S(2)}) copy-start(s32[64]{0:T(128)} %param.22) | copy-start | bytes 772
  30.7 203.2 %all-to-all-start = ((bf16[20,64,3584]{2,1,0:T(8,128)(2,1)}), bf16[20,64,3584]{2,1,0:T(8,128)(2,1)}, u32[]{:S(2)}, u32[]{:S(2)}) async-start(bf16[20,64,3584]{2,1,0:T(8,128)(2,1)} %select_select_fusion), calls=%async_computation | async-start | bytes 18350080 | tf_op jit(solution)/shard_map/all_to_all | solution.py:125
  37.0 316.2 %all-gather.8.cloned.1.call-start = ((), (), s32[]{:S(2)}) async-start(), calls=%async_computation.6 | async-start | bytes 14450688 | tf_op jit(solution)/shard_map/all_gather | solution.py:155
  233.9 18.7 %all-to-all-start.2 = ((bf16[16,8,3584]{2,1,0:T(8,128)(2,1)}), bf16[16,8,3584]{2,1,0:T(8,128)(2,1)S(1)}, u32[]{:S(2)}, u32[]{:S(2)}) async-start(bf16[16,8,3584]{2,1,0:T(8,128)(2,1)} %broadcast_select_fusion.2), calls=%async_computation.2 | async-start | bytes 1835008 | tf_op jit(solution)/shard_map/all_to_all | solution.py:133
  252.6 5.9 copy-start.3
  252.6 6.6 copy-start.12
  252.6 6.6 copy-start.5
  252.6 86.6 %all-to-all-start.1 = ((bf16[16,64,3584]{2,1,0:T(8,128)(2,1)}), bf16[16,64,3584]{2,1,0:T(8,128)(2,1)}, u32[]{:S(2)}, u32[]{:S(2)}) async-start(bf16[16,64,3584]{2,1,0:T(8,128)(2,1)} %broadcast_select_fusion), calls=%async_computation.1 | async-start | bytes 14680064 | tf_op jit(solution)/shard_map/all_to_all | solution.py:132
  339.2 3.8 copy-start.8
  343.0 6.1 copy-start.6
  343.0 2.9 copy-start.10
  348.3 1.5 copy-start.9
  477.2 6.5 copy-start.11
  489.3 5.9 copy-start.14
  489.3 5.9 copy-start.16
  489.3 5.9 copy-start.17
  489.3 6.0 copy-start.18
  489.3 48.0 %all-to-all-start.3 = ((bf16[2,512,1792]{2,0,1:T(2,128)(2,1)}), bf16[2,512,1792]{2,0,1:T(2,128)(2,1)}, u32[]{:S(2)}, u32[]{:S(2)}) async-start(bf16[2,512,1792]{2,0,1:T(2,128)(2,1)} %broadcast_select_fusion.1), calls=%async_computation.3 | async-start | bytes 7340032 | tf_op jit(solution)/shard_map/all_to_all | solution.py:176
  550.6 5.4 copy-start.19
  550.6 106.6 %copy-start.1 = (bf16[32,8,3584]{2,1,0:T(8,128)(2,1)S(1)}, bf16[32,8,3584]{2,1,0:T(8,128)(2,1)}, u32[]{:S(2)}) copy-start(bf16[32,8,3584]{2,1,0:T(8,128)(2,1)} %param.19) | copy-start | bytes 5505028
  551.0 51.6 %collective-permute-start = (bf16[5,64,1792]{2,1,0:T(8,128)(2,1)S(1)}, bf16[5,64,1792]{2,1,0:T(8,128)(2,1)S(1)}, u32[]{:S(2)}, u32[]{:S(2)}) collective-permute-start(bf16[5,64,1792]{2,1,0:T(8,128)(2,1)S(1)} %get-tuple-element.61), channel_id=1, source_target_pairs={{0,8},{8,0},{16,24},{24,16},{1,9},{9,1},{17,25},{25,17},{2,10},{10... | collective-permute-start | bytes 3440648 | tf_op jit(solution)/shard_map/ppermute | solution.py:28
  554.4 74.9 %collective-permute-start.1 = (bf16[5,64,1792]{2,1,0:T(8,128)(2,1)S(1)}, bf16[5,64,1792]{2,1,0:T(8,128)(2,1)S(1)}, u32[]{:S(2)}, u32[]{:S(2)}) collective-permute-start(bf16[5,64,1792]{2,1,0:T(8,128)(2,1)S(1)} %get-tuple-element.60), channel_id=1, source_target_pairs={{0,16},{8,24},{16,0},{24,8},{1,17},{9,25},{17,1},{25,9},{2,18},{10... | collective-permute-start | bytes 3440648 | tf_op jit(solution)/shard_map/ppermute | solution.py:28
  554.5 100.5 %collective-permute-start.2 = (bf16[5,64,1792]{2,1,0:T(8,128)(2,1)S(1)}, bf16[5,64,1792]{2,1,0:T(8,128)(2,1)S(1)}, u32[]{:S(2)}, u32[]{:S(2)}) collective-permute-start(bf16[5,64,1792]{2,1,0:T(8,128)(2,1)S(1)} %get-tuple-element.59), channel_id=1, source_target_pairs={{0,24},{8,16},{16,8},{24,0},{1,25},{9,17},{17,9},{25,1},{2,26},{10... | collective-permute-start | bytes 3440648 | tf_op jit(solution)/shard_map/ppermute | solution.py:28
  655.1 2.1 copy-start.7
Sparse Core Ops, SparseCore 0:
  9.9 27.8 all-gather.5
  39.6 26.6 all-gather.3
  68.2 73.0 all-gather.7
